TPU v7x, 256 devices: a whole 4x4x8 slice. The times are simulated.
256 devices in a mesh: row: 16 (over z, y_hi), col: 16 (over y_lo, x, core).
Axes of the slice: x: 4, y: 4 (y_hi: 2, y_lo: 2; y = y_hi * 2 + y_lo), z: 8, core: 2. Of those that a mesh axis runs over, the one named last changes fastest.
Arguments:
- amplitudes: bfloat16 [2048, 32768], P('row', 'col'), may hold values from -6 to 6
- amp_mask: int32 [64, 128], P('row', 'col'), may hold values from 0 to 1, as said below
- integrals: bfloat16 [16384, 32768], P('row', 'col'), may hold values from -0.0625 to 0.0625
- int_mask: int32 [64, 128], P('row', 'col'), may hold values 0 or 1
- occ_energy: float32 [2048], P('col'), may hold values from -1.5 to -0.5
- vir_energy: float32 [16384], P('row'), may hold values from 0.5 to 1.5
Outputs:
- residual: bfloat16 [2048, 16384], P('col', 'row')
Inputs may be any that keep to these rules, and one draw needn't show every extreme that they name: In every row of amp_mask, each aligned group of 8 consecutive entries holds exactly 4 ones.
All inputs are finite; a program needn't handle non-finite values. No bound on the sum of `int_mask` on one device may be relied on, other than what follows from the above.
Results may differ from a plain program's by a relative error of at most 0.001.
Values may be sent and summed in bfloat16 or wider, within the bound.
A program may use at most 64 MiB of HBM per device.

v0:
```python
import jax
import jax.numpy as jnp
from jax import lax
from jax.sharding import PartitionSpec as P

TILE = 256
IJ_BLK = 32


def expand_tiles(values, keep, rows_tile, cols_tile):
    nrow, ncol = keep.shape
    shaped = values.reshape(nrow, rows_tile, ncol, cols_tile)
    return (shaped * keep.astype(values.dtype)[:, None, :, None]).reshape(values.shape)


def contract(left, right):
    return lax.dot_general(
        left, right, (((1,), (1,)), ((), ())), preferred_element_type=jnp.float32
    )


def whole_sum(partial_value):
    return lax.psum_scatter(partial_value, "col", scatter_dimension=0, tiled=True)


def body(amplitudes, amp_mask, integrals, int_mask, occ_energy, vir_energy):
    int_used = expand_tiles(integrals, int_mask, TILE, TILE)
    amp_used = expand_tiles(amplitudes, amp_mask, IJ_BLK, TILE)
    partial_value = contract(lax.all_gather(amp_used, "row", axis=0, tiled=True), int_used)
    ladder = whole_sum(partial_value)
    denom = vir_energy[None, :] - occ_energy[:, None]
    return (ladder / denom).astype(jnp.bfloat16)


def solution(mesh):
    return jax.shard_map(
        body,
        mesh=mesh,
        in_specs=(
            P("row", "col"),
            P("row", "col"),
            P("row", "col"),
            P("row", "col"),
            P("col"),
            P("row"),
        ),
        out_specs=P("col", "row"),
        check_vma=False,
    )
```

profile of v0, /device:TPU:32, one launch (start us, length us, event | category | flops | bytes accessed | tf_op | source)
XLA Modules:
  0.0 246.6 jit_solution(13339371365637120035)
XLA Ops:
  6.5 0.0 all-gather.2.cloned.1.call-start
  6.5 0.7 convert_element_type.9
  7.2 0.1 mul.22
  7.3 0.1 copy.7
  7.5 2.0 mul.24
  9.5 0.0 all-gather.2.cloned.1.call-update
  9.5 0.0 reduce-scatter.2.cloned.1.call-start
  9.5 0.7 convert_element_type.10
  10.2 0.3 mul.25
  10.6 3.4 %copy.8 = bf16[128,8,8,256]{3,1,2,0:T(8,128)(2,1)} copy(bf16[128,8,8,256]{3,2,1,0:T(8,128)(2,1)S(1)} %bitcast.7) | data formatting | bytes 8388608
  14.0 132.0 %all-gather.2.cloned.1.call-done = bf16[2048,2048]{1,0:T(8,128)(2,1)} async-done(((bf16[128,2048]{1,0:T(8,128)(2,1)}), bf16[2048,2048]{1,0:T(8,128)(2,1)}) %all-gather.2.cloned.1.call-update) | async-done | bytes 8388624 | tf_op jit(solution)/shard_map/all_gather | solution.py:29
  146.0 15.8 %fusion = f32[2048,1024]{1,0:T(8,128)} fusion(bf16[2048,2048]{1,0:T(8,128)(2,1)} %all-gather.2.cloned.1.call-done, bf16[1024,2048]{1,0:T(8,128)(2,1)} %param.8, bf16[1024,2048]{1,0:T(8,128)(2,1)} %bitcast.8), kind=kOutput, calls=%fused_computation | convolution fusion | flops 8592031744 | bytes 25165824 | tf_op jit(solution)/shard_map/dot_general | solution.py:17
  161.8 0.0 copy-start
  161.8 0.0 copy-start.1
  161.8 0.0 reduce-scatter.2.cloned.1.call-update
  161.8 76.1 %reduce-scatter.2.cloned.1.call-done = f32[128,1024]{1,0:T(8,128)} async-done(((f32[2048,1024]{1,0:T(8,128)}), f32[128,1024]{1,0:T(8,128)}) %reduce-scatter.2.cloned.1.call-update) | async-done | bytes 524304 | tf_op jit(solution)/shard_map/reduce_scatter | solution.py:23
  237.9 0.0 copy-done
  237.9 0.0 copy-done.1
  237.9 1.9 divide_convert_fusion
Async XLA Ops:
  6.5 139.5 %all-gather.2.cloned.1.call-start = ((), (), s32[]{:S(2)}) async-start(), calls=%async_computation.1 | async-start | bytes 8912896 | tf_op jit(solution)/shard_map/all_gather | solution.py:29
  9.5 228.4 %reduce-scatter.2.cloned.1.call-start = ((), (), s32[]{:S(2)}) async-start(), calls=%async_computation.2 | async-start | bytes 8912896 | tf_op jit(solution)/shard_map/reduce_scatter | solution.py:23
  161.8 76.1 %copy-start = (f32[1024]{0:T(1024)S(1)}, f32[1024]{0:T(1024)}, u32[]{:S(2)}) copy-start(f32[1024]{0:T(1024)} %param.11) | copy-start | bytes 12292
  161.8 76.1 %copy-start.1 = (f32[128]{0:T(128)S(1)}, f32[128]{0:T(128)}, u32[]{:S(2)}) copy-start(f32[128]{0:T(128)} %param.10) | copy-start | bytes 1540
Sparse Core Ops, SparseCore 0:
  9.9 136.0 all-gather.1
  162.0 75.8 reduce-scatter.1
where the time goes:
time: 247 us
  waiting for transfers between devices  208 us (84%)
  matrix products  15.8 us (6%)
  between operations  13.4 us (5%)
  other arithmetic  5.27 us (2%)
  local copies, waits for them, and re-layouts  3.96 us (2%)
    all_gather x1, waiting for transfers between devices, body(): lax.all_gather(amp_used, 'row', axis=0, tiled=True)  132 us
    reduce_scatter x1, waiting for transfers between devices, whole_sum(): lax.psum_scatter(partial_value, 'col', scatter_dimension=0, tiled=True)  76.1 us
    dot_general x1, matrix products, contract(): lax.dot_general(left, right, (((1,), (1,)), ((), ())), preferred_element_...  15.8 us
  transfers between devices with their start and end apart: 2, of which 2 were waited for; matrix products, arithmetic and copies ran while one was open for 2% of the time, Pallas kernels for 0%

commit v1 on v0

--- a/solution.py
+++ b/solution.py
@@ -26,7 +26,12 @@
 def body(amplitudes, amp_mask, integrals, int_mask, occ_energy, vir_energy):
     int_used = expand_tiles(integrals, int_mask, TILE, TILE)
     amp_used = expand_tiles(amplitudes, amp_mask, IJ_BLK, TILE)
-    partial_value = contract(lax.all_gather(amp_used, "row", axis=0, tiled=True), int_used)
+    partial_value = contract(
+        jnp.concatenate(
+            lax.all_to_all(jnp.stack([amp_used] * lax.axis_size("row")), "row", 0, 0), axis=0
+        ),
+        int_used,
+    )
     ladder = whole_sum(partial_value)
     denom = vir_energy[None, :] - occ_energy[:, None]
     return (ladder / denom).astype(jnp.bfloat16)

time: 247 us -> 318 us (1.29)
  waiting for transfers between devices: 208 us -> 266 us
  starting transfers between devices: 0.04 us -> 11.4 us
  local copies, waits for them, and re-layouts: 3.96 us -> 8.25 us
    all_to_all x0 -> x1, waiting for transfers between devices: none -> 189 us  [body(): lax.all_to_all(jnp.stack([amp_used] * lax.axis_size('row')), 'row', 0, 0)]
    all_gather x1 -> x0, waiting for transfers between devices: 132 us -> none  [body(): lax.all_gather(amp_used, 'row', axis=0, tiled=True)]
    all_to_all x0 -> x1, starting transfers between devices: none -> 11.3 us  [body(): lax.all_to_all(jnp.stack([amp_used] * lax.axis_size('row')), 'row', 0, 0)]
    another operation x0 -> x1, local copies, waits for them, and re-layouts: none -> 4.28 us  [body(): jnp.stack([amp_used] * lax.axis_size('row'))]
  transfers between devices with their start and end apart: 2 -> 2, of which waited for: 2 -> 2; matrix products, arithmetic and copies ran while one was open for 2% -> 1% of each run, Pallas kernels for 0% -> 0%
where the time goes in v1:
time: 318 us
  waiting for transfers between devices  266 us (84%)
  matrix products  15.8 us (5%)
  between operations  13.4 us (4%)
  starting transfers between devices  11.4 us (4%)
  local copies, waits for them, and re-layouts  8.25 us (3%)
  other arithmetic  3.75 us (1%)
    all_to_all x1, waiting for transfers between devices, body(): lax.all_to_all(jnp.stack([amp_used] * lax.axis_size('row')), 'row', 0, 0)  189 us
    reduce_scatter x1, waiting for transfers between devices, whole_sum(): lax.psum_scatter(partial_value, 'col', scatter_dimension=0, tiled=True)  76.8 us
    dot_general x1, matrix products, contract(): lax.dot_general(left, right, (((1,), (1,)), ((), ())), preferred_element_...  15.8 us
    all_to_all x1, starting transfers between devices, body(): lax.all_to_all(jnp.stack([amp_used] * lax.axis_size('row')), 'row', 0, 0)  11.3 us
  transfers between devices with their start and end apart: 2, of which 2 were waited for; matrix products, arithmetic and copies ran while one was open for 1% of the time, Pallas kernels for 0%

profile of v1, /device:TPU:32, one launch (start us, length us, event | category | flops | bytes accessed | tf_op | source)
XLA Modules:
  0.0 318.2 jit_solution(4140144668496321058)
XLA Ops:
  6.5 0.7 convert_element_type.9
  7.2 0.1 mul.23
  7.3 0.1 copy.7
  7.4 1.2 mul.25
  8.6 4.3 %stack.3 = bf16[16,128,2048]{2,1,0:T(8,128)(2,1)} broadcast(bf16[128,2048]{1,0:T(8,128)(2,1)S(1)} %mul.25), dimensions={1,2} | broadcast | bytes 8912896 | tf_op jit(solution)/shard_map/stack | solution.py:31
  12.9 0.0 copy-start.1
  12.9 11.3 %all-to-all-start = ((bf16[16,128,2048]{2,1,0:T(8,128)(2,1)}), bf16[16,128,2048]{2,1,0:T(8,128)(2,1)}, u32[]{:S(2)}, u32[]{:S(2)}) async-start(bf16[16,128,2048]{2,1,0:T(8,128)(2,1)} %stack.3), calls=%async_computation | async-start | bytes 16777216 | tf_op jit(solution)/shard_map/all_to_all | solution.py:31
  24.3 0.0 reduce-scatter.2.cloned.1.call-start
  24.3 0.0 copy-done.1
  24.3 0.3 mul.26
  24.7 3.4 %copy.8 = bf16[128,8,8,256]{3,1,2,0:T(8,128)(2,1)} copy(bf16[128,8,8,256]{3,2,1,0:T(8,128)(2,1)S(1)} %bitcast.8) | data formatting | bytes 8388608
  28.1 188.7 %all-to-all-done = bf16[16,128,2048]{2,1,0:T(8,128)(2,1)} async-done(((bf16[16,128,2048]{2,1,0:T(8,128)(2,1)}), bf16[16,128,2048]{2,1,0:T(8,128)(2,1)}, u32[]{:S(2)}, u32[]{:S(2)}) %all-to-all-start) | async-done | bytes 8388640 | tf_op jit(solution)/shard_map/all_to_all | solution.py:31
  216.8 15.8 %fusion = f32[2048,1024]{1,0:T(8,128)} fusion(bf16[2048,2048]{1,0:T(8,128)(2,1)} %bitcast, bf16[1024,2048]{1,0:T(8,128)(2,1)} %param.8, bf16[1024,2048]{1,0:T(8,128)(2,1)} %bitcast.9), kind=kOutput, calls=%fused_computation | convolution fusion | flops 8592031744 | bytes 25165824 | tf_op jit(solution)/shard_map/dot_general | solution.py:17
  232.6 0.0 copy-start
  232.6 0.0 copy-start.2
  232.6 0.0 reduce-scatter.2.cloned.1.call-update
  232.6 76.8 %reduce-scatter.2.cloned.1.call-done = f32[128,1024]{1,0:T(8,128)} async-done(((f32[2048,1024]{1,0:T(8,128)}), f32[128,1024]{1,0:T(8,128)}) %reduce-scatter.2.cloned.1.call-update) | async-done | bytes 524304 | tf_op jit(solution)/shard_map/reduce_scatter | solution.py:23
  309.4 0.0 copy-done
  309.4 0.0 copy-done.2
  309.4 1.9 divide_convert_fusion
  (1 shorter events, 0.0 us)
Async XLA Ops:
  12.9 11.4 %copy-start.1 = (s32[4,8]{1,0:T(4,128)S(1)}, s32[4,8]{1,0:T(4,128)}, u32[]{:S(2)}) copy-start(s32[4,8]{1,0:T(4,128)} %param.9) | copy-start | bytes 388
  12.9 203.9 %all-to-all-start = ((bf16[16,128,2048]{2,1,0:T(8,128)(2,1)}), bf16[16,128,2048]{2,1,0:T(8,128)(2,1)}, u32[]{:S(2)}, u32[]{:S(2)}) async-start(bf16[16,128,2048]{2,1,0:T(8,128)(2,1)} %stack.3), calls=%async_computation | async-start | bytes 16777216 | tf_op jit(solution)/shard_map/all_to_all | solution.py:31
  24.3 285.2 %reduce-scatter.2.cloned.1.call-start = ((), (), s32[]{:S(2)}) async-start(), calls=%async_computation.2 | async-start | bytes 8912896 | tf_op jit(solution)/shard_map/reduce_scatter | solution.py:23
  232.6 76.8 %copy-start = (f32[1024]{0:T(1024)S(1)}, f32[1024]{0:T(1024)}, u32[]{:S(2)}) copy-start(f32[1024]{0:T(1024)} %param.11) | copy-start | bytes 12292
  232.6 76.8 %copy-start.2 = (f32[128]{0:T(128)S(1)}, f32[128]{0:T(128)}, u32[]{:S(2)}) copy-start(f32[128]{0:T(128)} %param.10) | copy-start | bytes 1540
Sparse Core Ops, SparseCore 0:
  232.8 76.6 reduce-scatter.1
